TPU v7x, 32 devices: a whole 2x2x4 slice. The times are simulated.
32 devices in a mesh: req: 8 (over y, x, core), mp: 4 (over z).
Axes of the slice: x: 2, y: 2, z: 4, core: 2. Of those that a mesh axis runs over, the one named last changes fastest.
Arguments:
- latents: bfloat16 [16, 1, 384, 416], P('req', None, 'mp'), may hold values from -12 to 12
- prior_frame_cache: bfloat16 [16, 2, 384, 416], P('req', None, 'mp'), may hold values from -6 to 6
- move_to: int32 [16], P('req'), may hold values from 0 to 15, as said below
- counts: int32 [8], P('req'), may hold values from 1 to 2, as said below
- norm_gain: bfloat16 [384], P('mp'), may hold values from 0.5 to 1.5
- conv_weight: bfloat16 [27, 384, 384], P(None, 'mp'), may hold values from -0.0625 to 0.0625
- conv_bias: float32 [384], P('mp'), may hold values from -1.5 to 1.5
Outputs:
- decoded: bfloat16 [16, 1, 384, 416], P('req', None, 'mp')
- new_cache: bfloat16 [16, 2, 384, 416], P('req', None, 'mp')
Inputs may be any that keep to these rules, and one draw needn't show every extreme that they name: move_to is a permutation of the slots; a stream's new slot lies on its old index of req or on the next or previous one, the last and first index being neighbours; every index hands exactly 1 stream to each neighbour and takes the same number back from it. `counts`: some index of req is full and some other holds a single stream.
All inputs are finite; a program needn't handle non-finite values.
Results may differ from a plain program's by a relative error of at most 0.0018.
Values may be sent and summed in bfloat16 or wider, within the bound.
A program may use at most 64 MiB of HBM per device.

v0:
```python
import jax
import jax.numpy as jnp
from jax import lax
from jax.sharding import PartitionSpec as P

SECTION_CHANNELS = 384
LATENT_COLUMNS = 104


def shifted_2(block, axis, distance):
    devices = range(lax.axis_size(axis))
    route = [((i - distance) % len(devices), i) for i in devices]
    return lax.ppermute(block, axis, route)


def apply_taps(running, shard_in, weights, row_width):
    frames = shard_in.shape[1] - 2
    pixels = shard_in.shape[3]
    padded = jnp.pad(shard_in, ((0, 0), (0, 0), (0, 0), (row_width + 1, row_width + 1)))
    column = jnp.arange(pixels + 2 * row_width) % row_width
    for step_x in range(3):
        inside = ((column + step_x - 1 >= 0) & (column + step_x - 1 < row_width)).astype(
            shard_in.dtype
        )
        shifted = padded[:, :, :, step_x : step_x + pixels + 2 * row_width] * inside
        for step_y in range(3):
            window = shifted[:, :, :, step_y * row_width : step_y * row_width + pixels]
            for step_t in range(3):
                running = running + jnp.einsum(
                    "oc,stcp->stop",
                    weights[step_t * 9 + step_y * 3 + step_x],
                    window[:, step_t : step_t + frames],
                    preferred_element_type=jnp.float32,
                )
    return running


def pack_slots(prior_frame_cache, chosen, target, capacity):
    ranking = jnp.cumsum(chosen.astype(jnp.int32)) - 1
    picker = (chosen[None, :] & (ranking[None, :] == jnp.arange(capacity)[:, None])).astype(
        jnp.bfloat16
    )
    blocks = jnp.einsum(
        "cs,sfkp->cfkp", picker, prior_frame_cache, preferred_element_type=jnp.float32
    ).astype(jnp.bfloat16)
    labels = (jnp.dot(picker.astype(jnp.float32), (target + 1).astype(jnp.float32)) - 1.0).astype(
        jnp.bfloat16
    )
    return (blocks, labels)


def migrate(prior_frame_cache, move_to):
    slot_count = prior_frame_cache.shape[0]
    member_slots = lax.axis_size("req")
    position = lax.axis_index("req")
    capacity = slot_count // 2
    device = move_to // slot_count
    target = move_to % slot_count
    offset = (device - position) % member_slots
    goes_right = offset == 1
    goes_left = offset == member_slots - 1
    stays_put = offset == 0
    blocks_right, labels_right = pack_slots(prior_frame_cache, goes_right, target, capacity)
    blocks_left, labels_left = pack_slots(prior_frame_cache, goes_left, target, capacity)
    from_left = shifted_2((blocks_right, labels_right), "req", 1)
    from_right = shifted_2((blocks_left, labels_left), "req", -1)
    sources = jnp.concatenate([prior_frame_cache, from_left[0], from_right[0]], axis=0)
    own_labels = jnp.where(stays_put, target, -1).astype(jnp.float32)
    labels = jnp.concatenate(
        [own_labels, from_left[1].astype(jnp.float32), from_right[1].astype(jnp.float32)]
    )
    placing = (labels[None, :] == jnp.arange(slot_count, dtype=jnp.float32)[:, None]).astype(
        jnp.bfloat16
    )
    return jnp.einsum("ns,sfkp->nfkp", placing, sources, preferred_element_type=jnp.float32).astype(
        jnp.bfloat16
    )


def normalize(values, squares, gains):
    scaled = (
        values.astype(jnp.float32)
        * lax.rsqrt(squares / SECTION_CHANNELS + 1e-06)
        * gains.astype(jnp.float32)[:, None]
    )
    return jax.nn.silu(scaled).astype(jnp.bfloat16)


def shards(latents, prior_frame_cache, move_to, counts, norm_gain, conv_weight, conv_bias):
    moved = migrate(prior_frame_cache, move_to)
    slot_count = latents.shape[0]
    frames = latents.shape[1]
    live = (jnp.arange(slot_count) < counts[0])[:, None, None, None]
    start_zero = jnp.zeros(
        (slot_count, frames, conv_weight.shape[1], latents.shape[3]), jnp.float32
    )
    values = latents.astype(jnp.float32)
    partial_squares = jnp.sum(values * values, axis=2, keepdims=True)
    squares = lax.psum(partial_squares, "mp")
    hidden = normalize(latents, squares, norm_gain)
    extended = jnp.concatenate([moved, hidden], axis=1)
    conv_sum = apply_taps(
        start_zero, lax.all_gather(extended, "mp", axis=2, tiled=True), conv_weight, LATENT_COLUMNS
    )
    total = latents.astype(jnp.float32) + conv_sum + conv_bias[:, None]
    decoded = jnp.where(live, total, jnp.zeros_like(total)).astype(jnp.bfloat16)
    new_cache = extended[:, frames:]
    return (decoded, new_cache)


def solution(mesh):
    in_specs = (
        P("req", None, "mp", None),
        P("req", None, "mp", None),
        P("req"),
        P("req"),
        P("mp"),
        P(None, "mp", None),
        P("mp"),
    )
    out_specs = (P("req", None, "mp", None), P("req", None, "mp", None))
    return jax.shard_map(shards, mesh=mesh, in_specs=in_specs, out_specs=out_specs, check_vma=False)
```

profile of v0, /device:TPU:0, one launch (start us, length us, event | category | flops | bytes accessed | tf_op | source)
XLA Modules:
  0.0 157.5 jit_solution(8122907851598073962)
XLA Ops:
  7.2 0.0 all-gather.2.cloned.1.call-start
  7.2 0.7 fusion.140
  7.9 0.2 reduce-window.18
  8.1 0.2 reduce-window.19
  8.3 0.6 select_reduce_fusion.1
  9.5 1.5 collective-permute-start
  11.7 4.0 %collective-permute-start.1 = (bf16[1]{0:T(256)(128)(2,1)}, bf16[1]{0:T(256)(128)(2,1)}, u32[]{:S(2)}, u32[]{:S(2)}) collective-permute-start(bf16[1]{0:T(256)(128)(2,1)} %bitcast.7), channel_id=1, source_target_pairs={{4,0},{8,4},{12,8},{16,12},{20,16},{24,20},{28,24},{0,28},{5,1},{9... | collective-permute-start | bytes 14 | tf_op jit(solution)/shard_map/ppermute | solution.py:13
  15.7 1.4 copy.130
  17.1 0.6 fusion.135
  17.6 0.0 copy-start.3
  17.6 0.0 copy-start.1
  17.7 0.3 copy.128
  18.0 0.1 collective-permute-start.2
  18.1 0.6 fusion.133
  18.7 0.3 copy.129
  19.0 2.7 %collective-permute-start.3 = (bf16[1,2,96,416]{3,0,2,1:T(2,128)(2,1)S(1)}, bf16[1,2,96,416]{3,0,2,1:T(2,128)(2,1)S(1)}, u32[]{:S(2)}, u32[]{:S(2)}) collective-permute-start(bf16[1,2,96,416]{3,0,2,1:T(2,128)(2,1)S(1)} %copy.129), channel_id=1, source_target_pairs={{4,0},{8,4},{12,8},{16,12},{20,16},{24,20},{28,24},{0,28},{5,1},{9... | collective-permute-start | bytes 479240 | tf_op jit(solution)/shard_map/ppermute | solution.py:13
  21.7 0.0 copy-done.3
  21.7 0.0 copy-done.1
  21.7 0.1 fusion.50
  21.7 12.7 %psum.7 = f32[2,1,1,416]{3,0,2,1:T(2,128)S(1)} all-reduce(f32[2,1,1,416]{3,0,2,1:T(2,128)S(1)} %bitcast.336), channel_id=1, replica_groups=mesh['req'=8,'mp'=4] {'mp'}, use_global_device_ids=true, to_apply=%region_3.4 | all-reduce | flops 832 | bytes 6656 | tf_op jit(solution)/shard_map/psum | solution.py:99
  34.5 0.2 fusion.57
  34.7 0.2 copy.131
  36.2 0.1 pad_maximum_fusion.3
  36.3 0.0 collective-permute-done.2
  36.3 0.0 collective-permute-done.3
  36.3 1.5 convolution_convert_fusion
  37.8 1.7 %pad_maximum_fusion.2 = bf16[2,3,96,416]{3,0,2,1:T(2,128)(2,1)} fusion(bf16[2,1,96,416]{3,0,2,1:T(2,128)(2,1)S(1)} %copy.131, bf16[2,2,96,416]{3,0,2,1:T(2,128)(2,1)S(1)} %convolution_convert_fusion), kind=kLoop, calls=%fused_computation.110 | loop fusion | flops 239616 | bytes 958464 | tf_op jit(solution)/shard_map/concatenate | solution.py:101
  39.5 0.0 all-gather.2.cloned.1.call-update
  40.2 0.6 fusion.49
  40.8 0.8 copy.160
  41.6 45.3 %all-gather.2.cloned.1.call-done = bf16[2,3,384,416]{3,0,2,1:T(2,128)(2,1)} async-done(((bf16[2,3,96,416]{3,0,2,1:T(2,128)(2,1)}), bf16[2,3,384,416]{3,0,2,1:T(2,128)(2,1)}) %all-gather.2.cloned.1.call-update) | async-done | bytes 1916944 | tf_op jit(solution)/shard_map/all_gather | solution.py:103
  87.0 18.8 %slice_multiply_fusion.2 = (bf16[2,3,384,624]{3,0,2,1:T(2,128)(2,1)S(1)}, bf16[2,3,384,624]{3,0,2,1:T(2,128)(2,1)S(1)}, bf16[2,3,384,624]{3,0,2,1:T(2,128)(2,1)S(1)}) fusion(bf16[624]{0:T(1024)(128)(2,1)S(1)} %fusion.127, bf16[2,3,384,416]{3,0,2,1:T(2,128)(2,1)} %all-gather.2.cloned.1.call-done, bf16[624]{0:T(1024)(128)(2,1)S(1)} %fusion.129, ...), kind=kLoop, calls=%fused_computation.2 | loop fusion | flops 17252352 | bytes 10546848 | tf_op jit(solution)/shard_map/mul | solution.py:25
  105.8 0.0 copy-start
  105.8 10.7 %slice_bitcast_fusion.18 = (bf16[2,384,416]{2,0,1:T(2,128)(2,1)S(1)}, bf16[2,384,416]{2,0,1:T(2,128)(2,1)S(1)}, bf16[2,384,416]{2,0,1:T(2,128)(2,1)S(1)}, bf16[2...) fusion(bf16[2,3,384,624]{3,0,2,1:T(2,128)(2,1)S(1)} %get-tuple-, ...), kind=kLoop, calls=%fused_computation.66 | loop fusion | bytes 11501568 | tf_op jit(solution)/shard_map/reshape.33
  116.5 0.3 fusion.47
  116.8 25.4 %slice_bitcast_fusion.8 = (bf16[2,384,416]{2,0,1:T(2,128)(2,1)S(1)}, bf16[2,384,416]{2,0,1:T(2,128)(2,1)S(1)}, bf16[2,384,416]{2,0,1:T(2,128)(2,1)S(1)}, bf16[2,...) fusion(bf16[2,3,384,624]{3,0,2,1:T(2,128)(2,1)S(1)} %get-tuple-, ...), kind=kLoop, calls=%fused_computation.56 | loop fusion | bytes 23003136 | tf_op jit(solution)/shard_map/reshape.53
  142.2 0.3 convolution_bitcast_fusion.8
  142.5 0.3 convolution_bitcast_fusion
  142.7 0.3 convolution_bitcast_fusion.1
  143.0 0.3 convolution_bitcast_fusion.2
  143.3 0.3 convolution_bitcast_fusion.3
  143.6 0.3 convolution_bitcast_fusion.4
  143.9 0.3 convolution_bitcast_fusion.5
  144.2 0.3 convolution_bitcast_fusion.6
  144.5 0.3 convolution_bitcast_fusion.7
  144.8 0.3 convolution_bitcast_fusion.9
  145.1 0.3 convolution_add_fusion.14
  145.4 0.3 convolution_add_fusion.13
  145.7 0.3 convolution_add_fusion.12
  145.9 0.3 convolution_add_fusion.11
  146.2 0.3 convolution_add_fusion.10
  146.5 0.3 convolution_add_fusion.9
  146.8 0.3 convolution_add_fusion.8
  147.1 0.3 convolution_add_fusion.7
  147.4 0.3 convolution_add_fusion.6
  147.7 0.3 convolution_add_fusion.5
  148.0 0.3 convolution_add_fusion.4
  148.3 0.3 convolution_add_fusion.3
  148.6 0.3 convolution_add_fusion.2
  148.9 0.0 copy-start.2
  148.9 0.3 convolution_add_fusion.1
  149.2 0.3 fusion
  149.5 0.1 copy-done.2
  149.6 1.1 fusion.17
  (12 shorter events, 0.1 us)
Async XLA Ops:
  7.2 79.8 %all-gather.2.cloned.1.call-start = ((), (), s32[]{:S(2)}) async-start(), calls=%async_computation | async-start | bytes 2949120 | tf_op jit(solution)/shard_map/all_gather | solution.py:103
  9.5 25.4 %collective-permute-start = (bf16[1]{0:T(256)(128)(2,1)}, bf16[1]{0:T(256)(128)(2,1)}, u32[]{:S(2)}, u32[]{:S(2)}) collective-permute-start(bf16[1]{0:T(256)(128)(2,1)} %bitcast.4), channel_id=1, source_target_pairs={{28,0},{0,4},{4,8},{8,12},{12,16},{16,20},{20,24},{24,28},{29,1},{... | collective-permute-start | bytes 14 | tf_op jit(solution)/shard_map/ppermute | solution.py:13
  11.7 23.9 %collective-permute-start.1 = (bf16[1]{0:T(256)(128)(2,1)}, bf16[1]{0:T(256)(128)(2,1)}, u32[]{:S(2)}, u32[]{:S(2)}) collective-permute-start(bf16[1]{0:T(256)(128)(2,1)} %bitcast.7), channel_id=1, source_target_pairs={{4,0},{8,4},{12,8},{16,12},{20,16},{24,20},{28,24},{0,28},{5,1},{9... | collective-permute-start | bytes 14 | tf_op jit(solution)/shard_map/ppermute | solution.py:13
  17.6 4.0 %copy-start.3 = (bf16[96]{0:T(256)(128)(2,1)S(1)}, bf16[96]{0:T(256)(128)(2,1)}, u32[]{:S(2)}) copy-start(bf16[96]{0:T(256)(128)(2,1)} %param.11) | copy-start | bytes 580
  17.6 4.0 %copy-start.1 = (bf16[2,1,96,416]{3,2,1,0:T(8,128)(2,1)S(1)}, bf16[2,1,96,416]{3,2,1,0:T(8,128)(2,1)}, u32[]{:S(2)}) copy-start(bf16[2,1,96,416]{3,2,1,0:T(8,128)(2,1)} %param.7) | copy-start | bytes 479236
  18.0 18.3 %collective-permute-start.2 = (bf16[1,2,96,416]{3,0,2,1:T(2,128)(2,1)S(1)}, bf16[1,2,96,416]{3,0,2,1:T(2,128)(2,1)S(1)}, u32[]{:S(2)}, u32[]{:S(2)}) collective-permute-start(bf16[1,2,96,416]{3,0,2,1:T(2,128)(2,1)S(1)} %copy.128), channel_id=1, source_target_pairs={{28,0},{0,4},{4,8},{8,12},{12,16},{16,20},{20,24},{24,28},{29,1},{... | collective-permute-start | bytes 479240 | tf_op jit(solution)/shard_map/ppermute | solution.py:13
  19.0 17.3 %collective-permute-start.3 = (bf16[1,2,96,416]{3,0,2,1:T(2,128)(2,1)S(1)}, bf16[1,2,96,416]{3,0,2,1:T(2,128)(2,1)S(1)}, u32[]{:S(2)}, u32[]{:S(2)}) collective-permute-start(bf16[1,2,96,416]{3,0,2,1:T(2,128)(2,1)S(1)} %copy.129), channel_id=1, source_target_pairs={{4,0},{8,4},{12,8},{16,12},{20,16},{24,20},{28,24},{0,28},{5,1},{9... | collective-permute-start | bytes 479240 | tf_op jit(solution)/shard_map/ppermute | solution.py:13
  105.8 10.7 %copy-start = (bf16[27,96,384]{2,1,0:T(8,128)(2,1)S(1)}, bf16[27,96,384]{2,1,0:T(8,128)(2,1)}, u32[]{:S(2)}) copy-start(bf16[27,96,384]{2,1,0:T(8,128)(2,1)} %param.12) | copy-start | bytes 5971972
  148.9 0.7 copy-start.2
Sparse Core Ops, SparseCore 0:
  39.7 47.2 all-gather.1
where the time goes:
time: 158 us
  waiting for transfers between devices  45.3 us (29%)
  local copies, waits for them, and re-layouts  39.2 us (25%)
  other arithmetic  23.1 us (15%)
  between operations  17.7 us (11%)
  blocking collectives  12.7 us (8%)
  matrix products  11.2 us (7%)
  starting transfers between devices  8.27 us (5%)
    all_gather x1, waiting for transfers between devices, shards(): lax.all_gather(extended, 'mp', axis=2, tiled=True)  45.3 us
    another operation x2, local copies, waits for them, and re-layouts  36.1 us
    mul x1, other arithmetic, apply_taps(): shifted = padded[:, :, :, step_x:step_x + pixels + 2 * row_width] * inside  18.8 us
    psum x1, blocking collectives, shards(): squares = lax.psum(partial_squares, 'mp')  12.7 us
    dot_general x27, matrix products, apply_taps(): jnp.einsum('oc,stcp->stop', weights[step_t * 9 + step_y * 3 + step_x], wi...  8.54 us
    ppermute x4, starting transfers between devices, shifted_2(): return lax.ppermute(block, axis, route)  8.23 us
  transfers between devices with their start and end apart: 5, of which 1 were waited for; matrix products, arithmetic and copies ran while one was open for 3% of the time, Pallas kernels for 0%

commit v1 on v0

--- a/solution.py
+++ b/solution.py
@@ -5,6 +5,23 @@
 
 SECTION_CHANNELS = 384
 LATENT_COLUMNS = 104
+
+
+def joined_along(pieces, dim):
+    pieces = jnp.moveaxis(pieces, 0, dim)
+    shape = pieces.shape
+    return pieces.reshape(*shape[:dim], shape[dim] * shape[dim + 1], *shape[dim + 2 :])
+
+
+def collect(array, axis, dim):
+    count = lax.axis_size(axis)
+    right = [(i, (i + 1) % count) for i in range(count)]
+    blocks = [array]
+    while len(blocks) < count:
+        blocks.append(lax.ppermute(blocks[-1], axis, right))
+    index = lax.axis_index(axis)
+    blocks = jnp.stack(blocks)[(index - jnp.arange(count)) % count]
+    return joined_along(blocks, dim)
 
 
 def shifted_2(block, axis, distance):
@@ -99,9 +116,7 @@
     squares = lax.psum(partial_squares, "mp")
     hidden = normalize(latents, squares, norm_gain)
     extended = jnp.concatenate([moved, hidden], axis=1)
-    conv_sum = apply_taps(
-        start_zero, lax.all_gather(extended, "mp", axis=2, tiled=True), conv_weight, LATENT_COLUMNS
-    )
+    conv_sum = apply_taps(start_zero, collect(extended, "mp", 2), conv_weight, LATENT_COLUMNS)
     total = latents.astype(jnp.float32) + conv_sum + conv_bias[:, None]
     decoded = jnp.where(live, total, jnp.zeros_like(total)).astype(jnp.bfloat16)
     new_cache = extended[:, frames:]

time: 158 us -> 106 us (0.67)
  the two profiles are of different devices: /device:TPU:0 before, /device:TPU:2 now
where the time goes in v1:
time: 106 us
  waiting for transfers between devices  41.9 us (40%)
  other arithmetic  15.7 us (15%)
  local copies, waits for them, and re-layouts  13.9 us (13%)
  matrix products  12.8 us (12%)
  blocking collectives  12 us (11%)
  starting transfers between devices  5.77 us (5%)
  between operations  4.16 us (4%)
    ppermute x3, waiting for transfers between devices, collect(): blocks.append(lax.ppermute(blocks[-1], axis, right))  41.9 us
    psum x1, blocking collectives, shards(): squares = lax.psum(partial_squares, 'mp')  12 us
    dot_general x27, matrix products, apply_taps(): jnp.einsum('oc,stcp->stop', weights[step_t * 9 + step_y * 3 + step_x], wi...  10.2 us
    another operation x2, other arithmetic, collect(): blocks = jnp.stack(blocks)[(index - jnp.arange(count)) % count]  6.54 us
    gather x1, local copies, waits for them, and re-layouts, collect(): blocks = jnp.stack(blocks)[(index - jnp.arange(count)) % count]  6.28 us
    ppermute x4, starting transfers between devices, shifted_2(): return lax.ppermute(block, axis, route)  5.71 us
    mul x1, other arithmetic, apply_taps(): shifted = padded[:, :, :, step_x:step_x + pixels + 2 * row_width] * inside  5.69 us
    reshape x1, local copies, waits for them, and re-layouts, joined_along(): pieces.reshape(*shape[:dim], shape[dim] * shape[dim + 1], *shape[dim + 2:])  2.37 us
  transfers between devices with their start and end apart: 7, of which 3 were waited for; matrix products, arithmetic and copies ran while one was open for 6% of the time, Pallas kernels for 0%

profile of v1, /device:TPU:2, one launch (start us, length us, event | category | flops | bytes accessed | tf_op | source)
XLA Modules:
  0.0 106.2 jit_solution(6733355435470318716)
XLA Ops:
  0.6 0.7 fusion.116
  1.3 0.2 reduce-window.18
  1.5 0.2 reduce-window.19
  1.7 0.6 select_reduce_fusion.1
  2.9 1.0 collective-permute-start
  4.6 0.0 copy-start.4
  4.6 0.0 copy-start.1
  4.6 2.9 %collective-permute-start.1 = (bf16[1]{0:T(256)(128)(2,1)}, bf16[1]{0:T(256)(128)(2,1)}, u32[]{:S(2)}, u32[]{:S(2)}) collective-permute-start(bf16[1]{0:T(256)(128)(2,1)} %bitcast.7), channel_id=1, source_target_pairs={{4,0},{8,4},{12,8},{16,12},{20,16},{24,20},{28,24},{0,28},{5,1},{9... | collective-permute-start | bytes 14 | tf_op jit(solution)/shard_map/ppermute | solution.py:30
  7.5 1.4 %copy.78 = bf16[2,2,96,416]{3,0,2,1:T(2,128)(2,1)S(1)} copy(bf16[2,2,96,416]{3,2,1,0:T(8,128)(2,1)} %param.8) | data formatting | bytes 638976 | tf_op args[1]
  8.9 0.6 fusion.111
  9.5 0.3 copy.76
  9.8 0.1 collective-permute-start.2
  9.9 0.6 fusion.109
  10.5 0.3 copy.77
  10.8 1.8 %collective-permute-start.3 = (bf16[1,2,96,416]{3,0,2,1:T(2,128)(2,1)S(1)}, bf16[1,2,96,416]{3,0,2,1:T(2,128)(2,1)S(1)}, u32[]{:S(2)}, u32[]{:S(2)}) collective-permute-start(bf16[1,2,96,416]{3,0,2,1:T(2,128)(2,1)S(1)} %copy.77), channel_id=1, source_target_pairs={{4,0},{8,4},{12,8},{16,12},{20,16},{24,20},{28,24},{0,28},{5,1},{9... | collective-permute-start | bytes 479240 | tf_op jit(solution)/shard_map/ppermute | solution.py:30
  12.6 0.1 fusion.26
  12.6 12.0 %psum.7 = f32[2,1,1,416]{3,0,2,1:T(2,128)S(1)} all-reduce(f32[2,1,1,416]{3,0,2,1:T(2,128)S(1)} %bitcast.377), channel_id=1, replica_groups=mesh['req'=8,'mp'=4] {'mp'}, use_global_device_ids=true, to_apply=%region_3.4 | all-reduce | flops 832 | bytes 6656 | tf_op jit(solution)/shard_map/psum | solution.py:116
  24.6 0.2 fusion.33
  24.8 0.2 copy.79
  26.4 0.1 pad_maximum_fusion.4
  26.5 0.0 collective-permute-done.2
  26.5 0.0 collective-permute-done.3
  26.5 1.5 %convolution_convert_fusion = bf16[2,2,96,416]{3,0,2,1:T(2,128)(2,1)S(1)} fusion(bf16[1,2,96,416]{3,0,2,1:T(2,128)(2,1)S(1)} %collective-permute-done.3, bf16[1,2,96,416]{3,0,2,1:T(2,128)(2,1)S(1)} %collective-permute-done.2, bf16[2,2,96,416]{3,0,2,1:T(2,128)(2,1)S(1)} %copy.78, f32[4]{0:T(128)S(1)} %pad_maximum_fusion.4), kind=kOutput, calls=%fused_computation.8 | convolution fusion | flops 3354632 | bytes 958480 | tf_op jit(solution)/shard_map/ns,sfkp->nfkp/dot_general | solution.py:92
  28.0 0.9 pad_maximum_fusion.3
  28.8 0.1 collective-permute-start.4
  28.9 15.8 %collective-permute-done.4 = bf16[2,3,96,416]{3,0,2,1:T(2,128)(2,1)S(1)} collective-permute-done((bf16[2,3,96,416]{3,0,2,1:T(2,128)(2,1)S(1)}, bf16[2,3,96,416]{3,0,2,1:T(2,128)(2,1)S(1)}, u32[]{:S(2)}, u32[]{:S(2)}) %collective-permute-start.4) | collective-permute-done | bytes 479264 | tf_op jit(solution)/shard_map/ppermute | solution.py:21
  45.4 14.3 %collective-permute-done.5 = bf16[2,3,96,416]{3,0,2,1:T(2,128)(2,1)S(1)} collective-permute-done((bf16[2,3,96,416]{3,0,2,1:T(2,128)(2,1)S(1)}, bf16[2,3,96,416]{3,0,2,1:T(2,128)(2,1)S(1)}, u32[]{:S(2)}, u32[]{:S(2)}) %collective-permute-start.5) | collective-permute-done | bytes 479264 | tf_op jit(solution)/shard_map/ppermute | solution.py:21
  59.7 0.6 fusion.25
  60.3 0.8 copy.83
  61.1 0.9 fusion.124
  62.0 11.8 %collective-permute-done.6 = bf16[2,3,96,416]{3,0,2,1:T(2,128)(2,1)S(1)} collective-permute-done((bf16[2,3,96,416]{3,0,2,1:T(2,128)(2,1)S(1)}, bf16[2,3,96,416]{3,0,2,1:T(2,128)(2,1)S(1)}, u32[]{:S(2)}, u32[]{:S(2)}) %collective-permute-start.6) | collective-permute-done | bytes 479264 | tf_op jit(solution)/shard_map/ppermute | solution.py:21
  73.8 5.7 %pad_maximum_fusion = bf16[4,2,3,96,416]{4,1,3,2,0:T(2,128)(2,1)S(1)} fusion(bf16[1,2,3,96,416]{4,1,3,2,0:T(2,128)(2,1)S(1)} %bitcast.376, bf16[1,2,3,96,416]{4,1,3,2,0:T(2,128)(2,1)} %bitcast.375, bf16[1,2,3,96,416]{4,1,3,2,0:T(2,128)(2,1)S(1)} %bitcast.374, bf16[1,2,3,96,416]{4,1,3,2,0:T(2,128)(2,1)S(1)} %fusion.124), kind=kLoop, calls=%fused_computation.7 | loop fusion | flops 2875392 | bytes 3833856 | tf_op jit(solution)/shard_map/stack | solution.py:23
  79.4 6.3 %gather_fusion = bf16[4,2,3,96,416]{4,1,3,2,0:T(2,128)(2,1)} fusion(bf16[4,2,3,96,416]{4,1,3,2,0:T(2,128)(2,1)S(1)} %pad_maximum_fusion, s32[1024]{0:T(1024)S(1)} %pad_clamp_fusion), kind=kCustom, calls=%fused_computation | custom fusion | bytes 3833872 | tf_op jit(solution)/shard_map/gather | solution.py:23
  85.7 2.1 %copy.80 = bf16[2,3,4,96,416]{4,3,2,1,0:T(8,128)(2,1)S(1)} copy(bf16[2,3,4,96,416]{4,0,3,1,2:T(2,128)(2,1)} %bitcast.372) | data formatting | bytes 3833856 | tf_op jit(solution)/shard_map/transpose | solution.py:11
  87.9 2.4 %copy.81 = bf16[2,3,384,416]{2,3,0,1:T(8,128)(2,1)} copy(bf16[2,3,384,416]{3,2,1,0:T(8,128)(2,1)S(1)} %bitcast.373) | data formatting | bytes 3833856 | tf_op jit(solution)/shard_map/reshape | solution.py:13
  90.2 5.7 %fusion = (bf16[2,3,384,624]{2,3,0,1:T(8,128)(2,1)S(1)}, bf16[2,3,384,624]{2,3,0,1:T(8,128)(2,1)S(1)}, bf16[2,3,384,624]{2,3,0,1:T(8,128)(2,1)S(1)}) fusion(bf16[2,3,384,416]{2,3,0,1:T(8,128)(2,1)} %copy.81, bf16[624]{0:T(1024)(128)(2,1)S(1)} %get-tuple-element.19, bf16[624]{0:T(1024)(128)(2,1)S(1)} %fusion.105, bf16[624]{0:T(1024)(128)(2,1)S(1)} %get-tuple-element.18), kind=kLoop, calls=%fused_computation.4 | loop fusion | flops 17252352 | bytes 10546848 | tf_op jit(solution)/shard_map/mul | solution.py:42
  96.0 0.3 convolution_bitcast_fusion
  96.3 0.3 convolution_bitcast_fusion.1
  96.6 0.3 convolution_bitcast_fusion.2
  97.0 0.3 convolution_bitcast_fusion.3
  97.3 0.3 convolution_bitcast_fusion.4
  97.7 0.3 convolution_bitcast_fusion.5
  98.0 0.3 convolution_bitcast_fusion.6
  98.4 0.3 convolution_bitcast_fusion.7
  98.7 0.3 convolution_bitcast_fusion.8
  99.1 0.3 fusion.24
  99.4 0.3 convolution_add_fusion.14
  99.8 0.4 convolution_add_fusion.13
  100.1 0.3 convolution_add_fusion.12
  100.5 0.3 convolution_add_fusion.11
  100.8 0.3 convolution_add_fusion.10
  101.2 0.4 convolution_add_fusion.9
  101.5 0.3 convolution_add_fusion.8
  101.9 0.4 convolution_add_fusion.7
  102.2 0.3 convolution_bitcast_fusion.9
  102.6 0.4 convolution_add_fusion.6
  102.9 0.4 convolution_add_fusion.5
  103.3 0.4 convolution_add_fusion.4
  103.6 0.0 copy-start.3
  103.6 0.3 convolution_add_fusion.3
  104.0 0.3 convolution_add_fusion.2
  104.3 0.3 convolution_add_fusion.1
  104.7 0.4 fusion.3
  105.0 1.2 %fusion.20 = bf16[2,1,96,416]{3,2,1,0:T(8,128)(2,1)} fusion(f32[2,1,96,416]{3,2,0,1:T(8,128)S(1)} %convolution_bitcast_fusion, f32[2,1,96,416]{3,2,0,1:T(8,128)S(1)} %convolution_bitcast_fusion.1, f32[2,1,96,416]{3,2,0,1:T(8,128)S(1)} %convolution_bitcast_fusion.2, f32[2,1,96,416]{3,2,0,1:T(8,128)S(1)} %convolution_bitcast_fusion.3, ...), kind=kOutput, calls=%fused_computation.52 | convolution fusion | flops 62619648 | bytes 5395456 | tf_op jit(solution)/shard_map/oc,stcp->stop/dot_general | solution.py:46
  (21 shorter events, 0.1 us)
Async XLA Ops:
  2.9 22.1 %collective-permute-start = (bf16[1]{0:T(256)(128)(2,1)}, bf16[1]{0:T(256)(128)(2,1)}, u32[]{:S(2)}, u32[]{:S(2)}) collective-permute-start(bf16[1]{0:T(256)(128)(2,1)} %bitcast.4), channel_id=1, source_target_pairs={{28,0},{0,4},{4,8},{8,12},{12,16},{16,20},{20,24},{24,28},{29,1},{... | collective-permute-start | bytes 14 | tf_op jit(solution)/shard_map/ppermute | solution.py:30
  4.6 8.0 %copy-start.4 = (bf16[96]{0:T(256)(128)(2,1)S(1)}, bf16[96]{0:T(256)(128)(2,1)}, u32[]{:S(2)}) copy-start(bf16[96]{0:T(256)(128)(2,1)} %param.11) | copy-start | bytes 580
  4.6 8.0 %copy-start.1 = (bf16[2,1,96,416]{3,2,1,0:T(8,128)(2,1)S(1)}, bf16[2,1,96,416]{3,2,1,0:T(8,128)(2,1)}, u32[]{:S(2)}) copy-start(bf16[2,1,96,416]{3,2,1,0:T(8,128)(2,1)} %param.7) | copy-start | bytes 479236
  4.6 21.1 %collective-permute-start.1 = (bf16[1]{0:T(256)(128)(2,1)}, bf16[1]{0:T(256)(128)(2,1)}, u32[]{:S(2)}, u32[]{:S(2)}) collective-permute-start(bf16[1]{0:T(256)(128)(2,1)} %bitcast.7), channel_id=1, source_target_pairs={{4,0},{8,4},{12,8},{16,12},{20,16},{24,20},{28,24},{0,28},{5,1},{9... | collective-permute-start | bytes 14 | tf_op jit(solution)/shard_map/ppermute | solution.py:30
  9.8 16.7 %collective-permute-start.2 = (bf16[1,2,96,416]{3,0,2,1:T(2,128)(2,1)S(1)}, bf16[1,2,96,416]{3,0,2,1:T(2,128)(2,1)S(1)}, u32[]{:S(2)}, u32[]{:S(2)}) collective-permute-start(bf16[1,2,96,416]{3,0,2,1:T(2,128)(2,1)S(1)} %copy.76), channel_id=1, source_target_pairs={{28,0},{0,4},{4,8},{8,12},{12,16},{16,20},{20,24},{24,28},{29,1},{... | collective-permute-start | bytes 479240 | tf_op jit(solution)/shard_map/ppermute | solution.py:30
  10.8 15.7 %collective-permute-start.3 = (bf16[1,2,96,416]{3,0,2,1:T(2,128)(2,1)S(1)}, bf16[1,2,96,416]{3,0,2,1:T(2,128)(2,1)S(1)}, u32[]{:S(2)}, u32[]{:S(2)}) collective-permute-start(bf16[1,2,96,416]{3,0,2,1:T(2,128)(2,1)S(1)} %copy.77), channel_id=1, source_target_pairs={{4,0},{8,4},{12,8},{16,12},{20,16},{24,20},{28,24},{0,28},{5,1},{9... | collective-permute-start | bytes 479240 | tf_op jit(solution)/shard_map/ppermute | solution.py:30
  28.8 15.9 %collective-permute-start.4 = (bf16[2,3,96,416]{3,0,2,1:T(2,128)(2,1)S(1)}, bf16[2,3,96,416]{3,0,2,1:T(2,128)(2,1)S(1)}, u32[]{:S(2)}, u32[]{:S(2)}) collective-permute-start(bf16[2,3,96,416]{3,0,2,1:T(2,128)(2,1)S(1)} %pad_maximum_fusion.3), channel_id=1, source_target_pairs={{0,1},{1,2},{2,3},{3,0},{4,5},{5,6},{6,7},{7,4},{8,9},{9,10},{10,1... | collective-permute-start | bytes 1437704 | tf_op jit(solution)/shard_map/ppermute | solution.py:21
  44.7 15.0 %collective-permute-start.5 = (bf16[2,3,96,416]{3,0,2,1:T(2,128)(2,1)S(1)}, bf16[2,3,96,416]{3,0,2,1:T(2,128)(2,1)S(1)}, u32[]{:S(2)}, u32[]{:S(2)}) collective-permute-start(bf16[2,3,96,416]{3,0,2,1:T(2,128)(2,1)S(1)} %collective-permute-done.4), channel_id=1, source_target_pairs={{0,1},{1,2},{2,3},{3,0},{4,5},{5,6},{6,7},{7,4},{8,9},{9,10},{10,1... | collective-permute-start | bytes 1437704 | tf_op jit(solution)/shard_map/ppermute | solution.py:21
  59.6 14.1 %copy-start.2 = (bf16[2,3,96,416]{3,0,2,1:T(2,128)(2,1)}, bf16[2,3,96,416]{3,0,2,1:T(2,128)(2,1)S(1)}, u32[]{:S(2)}) copy-start(bf16[2,3,96,416]{3,0,2,1:T(2,128)(2,1)S(1)} %collective-permute-done.5) | copy-start | bytes 1437700
  59.7 14.1 %collective-permute-start.6 = (bf16[2,3,96,416]{3,0,2,1:T(2,128)(2,1)S(1)}, bf16[2,3,96,416]{3,0,2,1:T(2,128)(2,1)S(1)}, u32[]{:S(2)}, u32[]{:S(2)}) collective-permute-start(bf16[2,3,96,416]{3,0,2,1:T(2,128)(2,1)S(1)} %collective-permute-done.5), channel_id=1, source_target_pairs={{0,1},{1,2},{2,3},{3,0},{4,5},{5,6},{6,7},{7,4},{8,9},{9,10},{10,1... | collective-permute-start | bytes 1437704 | tf_op jit(solution)/shard_map/ppermute | solution.py:21
  90.2 5.7 %copy-start = (bf16[27,96,384]{2,1,0:T(8,128)(2,1)S(1)}, bf16[27,96,384]{2,1,0:T(8,128)(2,1)}, u32[]{:S(2)}) copy-start(bf16[27,96,384]{2,1,0:T(8,128)(2,1)} %param.12) | copy-start | bytes 5971972
  103.6 1.4 %copy-start.3 = (f32[96]{0:T(128)S(1)}, f32[96]{0:T(128)}, u32[]{:S(2)}) copy-start(f32[96]{0:T(128)} %param.13) | copy-start | bytes 1156
